TPU v7x, 32 devices: a whole 2x2x4 slice. The times are simulated.
32 devices in a mesh: groups: 2 (over x), out: 16 (over z, y, core).
Axes of the slice: x: 2, y: 2, z: 4, core: 2. Of those that a mesh axis runs over, the one named last changes fastest.
Arguments:
- tokens: bfloat16 [256, 8192], P('groups', 'out'), parts along dimension 0, may hold values from -60 to 60, as said below
- grad_hidden: bfloat16 [256, 16384], P('groups', 'out'), parts along dimension 0, may hold values from -6 to 6
- w_gate: bfloat16 [8192, 16384], P(None, 'out'), may hold values from -0.0625 to 0.0625
- w_up: bfloat16 [8192, 16384], P(None, 'out'), may hold values from -0.0625 to 0.0625
- a_factors: bfloat16 [8192, 128], replicated, may hold values from -0.0625 to 0.0625
- b_factors: bfloat16 [2, 64, 16384], P(None, None, 'out'), may hold values from -0.75 to 0.75
- magnitudes: float32 [2, 16384], P(None, 'out'), may hold values from 1 to 2
Outputs:
- hidden: bfloat16 [256, 16384], P('groups', 'out'), parts along dimension 0
- grad_tokens: bfloat16 [256, 8192], P('groups', 'out'), parts along dimension 0
- step_a: float32 [16384, 128], P(('groups', 'out')), parts along dimension 0
- step_b: float32 [4, 64, 16384], P('groups', None, 'out'), parts along dimension 0
- step_m: float32 [4, 16384], P('groups', 'out'), parts along dimension 0
There are 2 independent parts, one for each index of `groups`. A program takes and returns all parts, laid end to end along the dimension named above; an argument that names none is the same for every part. Nothing has to cross between parts.
Inputs may be any that keep to these rules, and one draw needn't show every extreme that they name: `tokens`: activations with feature scales that differ between features.
All inputs are finite; a program needn't handle non-finite values.
Results may differ from a plain program's by a relative error of at most 0.0073.
Values may be sent and summed in bfloat16 or wider, within the bound.
A program may use at most 128 MiB of HBM per device.

v0:
```python
import jax
import jax.numpy as jnp
from jax import lax
from jax.sharding import PartitionSpec as P

D = 8192
FW = 16384
R = 64


def inner_product(left_side, right_side, precision=None):
    return lax.dot_general(
        left_side,
        right_side,
        (((0,), (0,)), ((), ())),
        precision=precision,
        preferred_element_type=jnp.float32,
    )


def outer_contract(left_side, right_side, precision=None):
    return lax.dot_general(
        left_side,
        right_side,
        (((1,), (1,)), ((), ())),
        precision=precision,
        preferred_element_type=jnp.float32,
    )


def split_parts(values):
    upper = values.astype(jnp.bfloat16)
    lower = (values - upper.astype(jnp.float32)).astype(jnp.bfloat16)
    return (upper, lower)


def per_device(tokens, grad_hidden, w_gate, w_up, a_factors, b_factors, magnitudes):
    weights = (w_gate, w_up)
    rank = a_factors.shape[1] // 2
    count_tokens = tokens.shape[0]
    norms = []
    scales = []
    for which in range(2):
        weight = weights[which]
        left = a_factors[:, which * rank : (which + 1) * rank]
        right = b_factors[which]
        merged = weight.astype(jnp.float32) + jnp.dot(
            left, right, preferred_element_type=jnp.float32
        )
        squares = jnp.sum(merged * merged, axis=0)
        norm_col = jnp.sqrt(squares + 1e-06)
        norms.append(norm_col)
        scales.append(magnitudes[which] / norm_col)
    whole = lax.all_gather(tokens, "out", axis=1, tiled=True)
    base_gate = jnp.dot(whole, w_gate, preferred_element_type=jnp.float32)
    base_up = jnp.dot(whole, w_up, preferred_element_type=jnp.float32)
    low_wide = jnp.dot(whole, a_factors, preferred_element_type=jnp.float32)
    low = low_wide.astype(jnp.bfloat16)
    bases = []
    pres = []
    for which, raw in enumerate((base_gate, base_up)):
        base = raw + jnp.dot(
            low[:, which * rank : (which + 1) * rank],
            b_factors[which],
            preferred_element_type=jnp.float32,
        )
        bases.append(base)
        pres.append(base * scales[which][None, :])
    sigma = jax.nn.sigmoid(pres[0])
    hidden = (pres[0] * sigma * pres[1]).astype(jnp.bfloat16)
    cotangent = grad_hidden.astype(jnp.float32)
    dpres = (
        cotangent * pres[1] * sigma * (1.0 + pres[0] * (1.0 - sigma)),
        cotangent * pres[0] * sigma,
    )
    partial_sum = jnp.zeros((count_tokens, w_gate.shape[0]), jnp.float32)
    z_blocks = []
    grad_bs = []
    grad_ms = []
    for which in range(2):
        dscaled = (dpres[which] * scales[which][None, :]).astype(jnp.bfloat16)
        grad_ms.append(jnp.sum(dpres[which] * bases[which], axis=0) / norms[which])
        grad_bs.append(inner_product(low[:, which * rank : (which + 1) * rank], dscaled))
        z_blocks.append(outer_contract(dscaled, b_factors[which]))
        partial_sum = partial_sum + outer_contract(dscaled, weights[which])
    z_local = jnp.concatenate(z_blocks, axis=1)
    grad_b = jnp.stack(grad_bs)
    grad_m = jnp.stack(grad_ms)
    summed_inputs = lax.psum_scatter(partial_sum, "out", scatter_dimension=1, tiled=True)
    local_energy = jnp.sum(grad_b * grad_b) + jnp.sum(grad_m * grad_m)
    z_all, small_energy = lax.psum((z_local, local_energy), "out")
    z_upper, z_lower = split_parts(z_all)
    full_a = inner_product(whole, z_upper) + inner_product(whole, z_lower)
    grad_a = inner_product(tokens, z_upper) + inner_product(tokens, z_lower)
    mine = tokens.shape[1]
    a_mine = lax.dynamic_slice_in_dim(a_factors, lax.axis_index("out") * mine, mine, 0)
    adapter = outer_contract(z_upper, a_mine) + outer_contract(z_lower, a_mine)
    grad_tokens = (summed_inputs + adapter).astype(jnp.bfloat16)
    energy = small_energy + jnp.sum(full_a * full_a)
    count_all = 2 * D * R + 2 * R * FW + 2 * FW
    rms_value = jnp.sqrt(energy / count_all + 1e-06)
    return (hidden, grad_tokens, grad_a / rms_value, grad_b / rms_value, grad_m / rms_value)


def solution(mesh):
    in_specs = (
        P("groups", "out"),
        P("groups", "out"),
        P(None, "out"),
        P(None, "out"),
        P(),
        P(None, None, "out"),
        P(None, "out"),
    )
    out_specs = (
        P("groups", "out"),
        P("groups", "out"),
        P(("groups", "out"), None),
        P("groups", None, "out"),
        P("groups", "out"),
    )
    return jax.shard_map(
        per_device, mesh=mesh, in_specs=in_specs, out_specs=out_specs, check_vma=False
    )
```

profile of v0, /device:TPU:0, one launch (start us, length us, event | category | flops | bytes accessed | tf_op | source)
XLA Modules:
  0.0 256.2 jit_solution(1929650667966069490)
XLA Ops:
  7.2 0.7 all-gather.2.cloned.1.call-update
  8.0 8.9 %multiply_reduce_fusion.1 = f32[1024]{0:T(1024)S(1)} fusion(bf16[8192,1024]{1,0:T(8,128)(2,1)} %param.9, bf16[8192,128]{1,0:T(8,128)(2,1)} %param.11, bf16[2,64,1024]{2,1,0:T(8,128)(2,1)} %param.12), kind=kOutput, calls=%fused_computation.1 | convolution fusion | flops 1107295232 | bytes 19009536 | tf_op jit(solution)/shard_map/dot_general | solution.py:47
  16.9 2.9 %copy-done = bf16[8192,1024]{1,0:T(8,128)(2,1)S(1)} copy-done((bf16[8192,1024]{1,0:T(8,128)(2,1)S(1)}, bf16[8192,1024]{1,0:T(8,128)(2,1)}, u32[]{:S(2)}) %copy-start) | copy-done | bytes 16777240
  19.8 5.5 %multiply_reduce_fusion = f32[1024]{0:T(1024)S(1)} fusion(bf16[8192,1024]{1,0:T(8,128)(2,1)S(1)} %copy-done, bf16[8192,128]{1,0:T(8,128)(2,1)S(1)} %copy-done.2, bf16[2,64,1024]{2,1,0:T(8,128)(2,1)S(1)} %copy-done.3), kind=kOutput, calls=%fused_computation | convolution fusion | flops 1107295232 | bytes 19009536 | tf_op jit(solution)/shard_map/dot_general | solution.py:47
  25.4 28.7 %all-gather.2.cloned.1.call-done = bf16[128,8192]{1,0:T(8,128)(2,1)} async-done(((bf16[128,512]{1,0:T(8,128)(2,1)}), bf16[128,8192]{1,0:T(8,128)(2,1)}) %all-gather.2.cloned.1.call-update) | async-done | bytes 2097168 | tf_op jit(solution)/shard_map/all_gather | solution.py:54
  54.1 2.7 %convolution_convert_fusion = bf16[128,128]{0,1:T(8,128)(2,1)S(1)} fusion(bf16[128,8192]{1,0:T(8,128)(2,1)} %all-gather.2.cloned.1.call-done, bf16[8192,128]{1,0:T(8,128)(2,1)S(1)} %copy-done.2), kind=kOutput, calls=%fused_computation.18 | convolution fusion | flops 268451840 | bytes 4227072 | tf_op jit(solution)/shard_map/dot_general | solution.py:57
  56.8 8.9 %fusion.36 = f32[128,1024]{1,0:T(8,128)S(1)} fusion(bf16[128,8192]{1,0:T(8,128)(2,1)} %all-gather.2.cloned.1.call-done, bf16[8192,1024]{1,0:T(8,128)(2,1)} %param.10), kind=kOutput, calls=%fused_computation.66 | convolution fusion | flops 2147483648 | bytes 19398656 | tf_op jit(solution)/shard_map/dot_general | solution.py:56
  65.7 0.3 convolution_add_fusion.2
  66.0 0.8 slice-done.3
  66.8 0.6 copy-done.1
  67.4 2.5 fusion.35
  69.9 1.3 multiply_reduce_fusion.3
  71.2 0.2 fusion.16
  71.4 13.2 %fusion.37 = f32[128,8192]{1,0:T(8,128)} fusion(bf16[128,1024]{1,0:T(8,128)(2,1)S(1)} %get-tuple-element.14, bf16[8192,1024]{1,0:T(8,128)(2,1)} %param.9), kind=kOutput, calls=%fused_computation.67 | convolution fusion | flops 2147483648 | bytes 21233664 | tf_op jit(solution)/shard_map/dot_general | solution.py:22
  84.7 0.2 fusion.12
  84.9 0.6 pad_maximum_fusion.1
  85.6 0.3 reduce-scatter.2.cloned.1.call-start
  85.8 14.5 %convolution_add_fusion.1 = f32[128,8192]{1,0:T(8,128)} fusion(f32[128,8192]{1,0:T(8,128)} %fusion.37, bf16[128,1024]{1,0:T(8,128)(2,1)S(1)} %get-tuple-element.16, bf16[8192,1024]{1,0:T(8,128)(2,1)} %param.10), kind=kOutput, calls=%fused_computation.4 | convolution fusion | flops 2148532224 | bytes 25427968 | tf_op jit(solution)/shard_map/dot_general | solution.py:22
  100.4 0.6 multiply_reduce_fusion.5
  101.4 0.7 multiply_reduce_fusion.4
  103.4 32.1 %psum.15 = f32[]{:T(128)} all-reduce(f32[]{:T(128)S(6)} %add.96), channel_id=1, replica_groups=mesh['groups'=2,'out'=16] {'out'}, use_global_device_ids=true, to_apply=%region_8.0 | all-reduce | flops 1 | bytes 8 | tf_op jit(solution)/shard_map/psum | solution.py:91
  135.5 33.7 %all-reduce.2.cloned.1.call-done = f32[128,128]{0,1:T(8,128)} async-done(((f32[128,128]{0,1:T(8,128)}), f32[128,128]{0,1:T(8,128)}) %all-reduce.2.cloned.1.call-update) | async-done | bytes 65552 | tf_op jit(solution)/shard_map/psum | solution.py:91
  169.2 0.9 subtract_convert_fusion
  170.1 0.7 fusion.39
  170.8 1.9 fusion.3
  174.3 0.2 fusion.5
  174.5 0.8 copy.12
  175.3 0.6 broadcast_divide_fusion
  175.9 0.9 fusion.11
  176.8 1.1 fusion.21
  177.9 69.9 %reduce-scatter.2.cloned.1.call-done = f32[128,512]{1,0:T(8,128)} async-done(((f32[128,8192]{1,0:T(8,128)}), f32[128,512]{1,0:T(8,128)}) %reduce-scatter.2.cloned.1.call-update) | async-done | bytes 262160 | tf_op jit(solution)/shard_map/reduce_scatter | solution.py:89
  247.8 1.9 fusion.7
  (32 shorter events, 0.7 us)
Async XLA Ops:
  7.2 46.9 %all-gather.2.cloned.1.call-start = ((), (), s32[]{:S(2)}) async-start(), calls=%async_computation.1 | async-start | bytes 2228224 | tf_op jit(solution)/shard_map/all_gather | solution.py:54
  7.9 9.0 %copy-start.2 = (bf16[8192,128]{1,0:T(8,128)(2,1)S(1)}, bf16[8192,128]{1,0:T(8,128)(2,1)}, u32[]{:S(2)}) copy-start(bf16[8192,128]{1,0:T(8,128)(2,1)} %param.11) | copy-start | bytes 6291460
  7.9 9.0 %copy-start.3 = (bf16[2,64,1024]{2,1,0:T(8,128)(2,1)S(1)}, bf16[2,64,1024]{2,1,0:T(8,128)(2,1)}, u32[]{:S(2)}) copy-start(bf16[2,64,1024]{2,1,0:T(8,128)(2,1)} %param.12) | copy-start | bytes 786436
  7.9 161.3 %all-reduce.2.cloned.1.call-start = ((), (), s32[]{:S(2)}) async-start(), calls=%async_computation.3 | async-start | bytes 131072 | tf_op jit(solution)/shard_map/psum | solution.py:91
  8.0 11.9 %copy-start = (bf16[8192,1024]{1,0:T(8,128)(2,1)S(1)}, bf16[8192,1024]{1,0:T(8,128)(2,1)}, u32[]{:S(2)}) copy-start(bf16[8192,1024]{1,0:T(8,128)(2,1)} %param.10) | copy-start | bytes 50331652
  19.8 5.5 %copy-start.5 = (f32[2,1024]{1,0:T(2,128)S(1)}, f32[2,1024]{1,0:T(2,128)}, u32[]{:S(2)}) copy-start(f32[2,1024]{1,0:T(2,128)} %param.13) | copy-start | bytes 24580
  54.1 11.9 %slice-start = ((s8[16777216]{0:T(1024)(128)(4,1)}), s8[4194304]{0:T(1024)(128)(4,1)S(1)}, s32[]{:S(2)}) async-start(s8[16777216]{0:T(1024)(128)(4,1)} %bitcast.52), calls=%async_computation.4 | async-start | bytes 8388608
  56.8 9.2 %slice-start.1 = ((s8[16777216]{0:T(1024)(128)(4,1)}), s8[4194304]{0:T(1024)(128)(4,1)S(1)}, s32[]{:S(2)}) async-start(s8[16777216]{0:T(1024)(128)(4,1)} %bitcast.52), calls=%async_computation.5 | async-start | bytes 8388608
  56.8 9.2 %slice-start.2 = ((s8[16777216]{0:T(1024)(128)(4,1)}), s8[4194304]{0:T(1024)(128)(4,1)S(1)}, s32[]{:S(2)}) async-start(s8[16777216]{0:T(1024)(128)(4,1)} %bitcast.52), calls=%async_computation.6 | async-start | bytes 8388608
  56.8 10.0 %slice-start.3 = ((s8[16777216]{0:T(1024)(128)(4,1)}), s8[4194304]{0:T(1024)(128)(4,1)S(1)}, s32[]{:S(2)}) async-start(s8[16777216]{0:T(1024)(128)(4,1)} %bitcast.52), calls=%async_computation.7 | async-start | bytes 8388608
  56.8 10.6 %copy-start.1 = (bf16[128,8192]{1,0:T(8,128)(2,1)S(1)}, bf16[128,8192]{1,0:T(8,128)(2,1)}, u32[]{:S(2)}) copy-start(bf16[128,8192]{1,0:T(8,128)(2,1)} %all-gather.2.cloned.1.call-done) | copy-start | bytes 6291460
  67.4 2.5 copy-start.6
  85.6 162.2 %reduce-scatter.2.cloned.1.call-start = ((), (), s32[]{:S(2)}) async-start(), calls=%async_computation.2 | async-start | bytes 4456448 | tf_op jit(solution)/shard_map/reduce_scatter | solution.py:89
  170.8 3.3 %copy-start.4 = (bf16[128,512]{1,0:T(8,128)(2,1)S(1)}, bf16[128,512]{1,0:T(8,128)(2,1)}, u32[]{:S(2)}) copy-start(bf16[128,512]{1,0:T(8,128)(2,1)} %param.7) | copy-start | bytes 393220
Sparse Core Ops, SparseCore 0:
  10.2 43.8 all-gather.1
  85.7 83.4 all-reduce.1
  173.6 74.2 reduce-scatter.1
where the time goes:
time: 257 us; the launch traced here: 256 us
  waiting for transfers between devices  133 us (52%)
  matrix products  64.5 us (25%)
  blocking collectives  32.1 us (12%)
  between operations  16.7 us (6%)
  local copies, waits for them, and re-layouts  5.16 us (2%)
  other arithmetic  4.41 us (2%)
    reduce_scatter x1, waiting for transfers between devices, per_device(): lax.psum_scatter(partial_sum, 'out', scatter_dimension=1, tiled=True)  69.9 us
    psum x1, waiting for transfers between devices, per_device(): z_all, small_energy = lax.psum((z_local, local_energy), 'out')  33.7 us
    psum x1, blocking collectives, per_device(): z_all, small_energy = lax.psum((z_local, local_energy), 'out')  32.1 us
    dot_general x6, matrix products, outer_contract(): lax.dot_general(left_side, right_side, (((1,), (1,)), ((), ())), precisio...  31.2 us
    all_gather x1, waiting for transfers between devices, per_device(): whole = lax.all_gather(tokens, 'out', axis=1, tiled=True)  28.7 us
    dot_general x2, matrix products, per_device(): jnp.dot(left, right, preferred_element_type=jnp.float32)  14.4 us
    dot_general x1, matrix products, per_device(): base_up = jnp.dot(whole, w_up, preferred_element_type=jnp.float32)  8.88 us
    unnamed x23, local copies, waits for them, and re-layouts  5.16 us
  transfers between devices with their start and end apart: 3, of which 3 were waited for; matrix products, arithmetic and copies ran while one was open for 15% of the time, Pallas kernels for 0%

commit v1 on v0

--- a/solution.py
+++ b/solution.py
@@ -51,7 +51,12 @@
         norm_col = jnp.sqrt(squares + 1e-06)
         norms.append(norm_col)
         scales.append(magnitudes[which] / norm_col)
-    whole = lax.all_gather(tokens, "out", axis=1, tiled=True)
+    ring = [tokens]
+    for hop in range(15):
+        ring.append(lax.ppermute(ring[-1], "out", [(dev, (dev + 1) % 16) for dev in range(16)]))
+    whole = jnp.roll(
+        jnp.concatenate(ring[::-1], axis=1), (lax.axis_index("out") + 1) * ring[0].shape[1], axis=1
+    )
     base_gate = jnp.dot(whole, w_gate, preferred_element_type=jnp.float32)
     base_up = jnp.dot(whole, w_up, preferred_element_type=jnp.float32)
     low_wide = jnp.dot(whole, a_factors, preferred_element_type=jnp.float32)

time: 257 us -> 336 us (1.31)
  waiting for transfers between devices: 133 us -> 198 us
  local copies, waits for them, and re-layouts: 5.16 us -> 20 us
    ppermute x0 -> x15, waiting for transfers between devices: none -> 95.1 us  [per_device(): lax.ppermute(ring[-1], 'out', [(dev, (dev + 1) % 16) for dev in range(16)])]
    all_gather x1 -> x0, waiting for transfers between devices: 28.7 us -> none  [per_device(): whole = lax.all_gather(tokens, 'out', axis=1, tiled=True)]
    unnamed x23 -> x88, local copies, waits for them, and re-layouts: 5.16 us -> 20 us
  transfers between devices with their start and end apart: 3 -> 17, of which waited for: 3 -> 16; matrix products, arithmetic and copies ran while one was open for 15% -> 12% of each run, Pallas kernels for 0% -> 0%
where the time goes in v1:
time: 336 us; the launch traced here: 335 us
  waiting for transfers between devices  198 us (59%)
  matrix products  64.1 us (19%)
  blocking collectives  30 us (9%)
  local copies, waits for them, and re-layouts  20 us (6%)
  between operations  17.3 us (5%)
  other arithmetic  4.41 us (1%)
    ppermute x15, waiting for transfers between devices, per_device(): lax.ppermute(ring[-1], 'out', [(dev, (dev + 1) % 16) for dev in range(16)])  95.1 us
    reduce_scatter x1, waiting for transfers between devices, per_device(): lax.psum_scatter(partial_sum, 'out', scatter_dimension=1, tiled=True)  68.8 us
    psum x1, waiting for transfers between devices, per_device(): z_all, small_energy = lax.psum((z_local, local_energy), 'out')  34.4 us
    dot_general x6, matrix products, outer_contract(): lax.dot_general(left_side, right_side, (((1,), (1,)), ((), ())), precisio...  30.4 us
    psum x1, blocking collectives, per_device(): z_all, small_energy = lax.psum((z_local, local_energy), 'out')  30 us
    unnamed x88, local copies, waits for them, and re-layouts  20 us
    dot_general x2, matrix products, per_device(): jnp.dot(left, right, preferred_element_type=jnp.float32)  14.2 us
    dot_general x1, matrix products, per_device(): base_up = jnp.dot(whole, w_up, preferred_element_type=jnp.float32)  9.36 us
  transfers between devices with their start and end apart: 17, of which 16 were waited for; matrix products, arithmetic and copies ran while one was open for 12% of the time, Pallas kernels for 0%

profile of v1, /device:TPU:0, one launch (start us, length us, event | category | flops | bytes accessed | tf_op | source)
XLA Modules:
  0.0 335.0 jit_solution(2590636093917602862)
XLA Ops:
  7.7 7.9 %collective-permute-done = bf16[128,512]{1,0:T(8,128)(2,1)S(1)} collective-permute-done((bf16[128,512]{1,0:T(8,128)(2,1)}, bf16[128,512]{1,0:T(8,128)(2,1)S(1)}, u32[]{:S(2)}, u32[]{:S(2)}) %collective-permute-start) | collective-permute-done | bytes 131104 | tf_op jit(solution)/shard_map/ppermute | solution.py:56
  15.6 7.1 %collective-permute-done.1 = bf16[128,512]{1,0:T(8,128)(2,1)S(1)} collective-permute-done((bf16[128,512]{1,0:T(8,128)(2,1)S(1)}, bf16[128,512]{1,0:T(8,128)(2,1)S(1)}, u32[]{:S(2)}, u32[]{:S(2)}) %collective-permute-start.1) | collective-permute-done | bytes 131104 | tf_op jit(solution)/shard_map/ppermute | solution.py:56
  22.7 7.1 %collective-permute-done.2 = bf16[128,512]{1,0:T(8,128)(2,1)S(1)} collective-permute-done((bf16[128,512]{1,0:T(8,128)(2,1)S(1)}, bf16[128,512]{1,0:T(8,128)(2,1)S(1)}, u32[]{:S(2)}, u32[]{:S(2)}) %collective-permute-start.2) | collective-permute-done | bytes 131104 | tf_op jit(solution)/shard_map/ppermute | solution.py:56
  30.4 7.1 %collective-permute-done.3 = bf16[128,512]{1,0:T(8,128)(2,1)S(1)} collective-permute-done((bf16[128,512]{1,0:T(8,128)(2,1)S(1)}, bf16[128,512]{1,0:T(8,128)(2,1)S(1)}, u32[]{:S(2)}, u32[]{:S(2)}) %collective-permute-start.3) | collective-permute-done | bytes 131104 | tf_op jit(solution)/shard_map/ppermute | solution.py:56
  38.2 7.1 %collective-permute-done.4 = bf16[128,512]{1,0:T(8,128)(2,1)S(1)} collective-permute-done((bf16[128,512]{1,0:T(8,128)(2,1)S(1)}, bf16[128,512]{1,0:T(8,128)(2,1)S(1)}, u32[]{:S(2)}, u32[]{:S(2)}) %collective-permute-start.4) | collective-permute-done | bytes 131104 | tf_op jit(solution)/shard_map/ppermute | solution.py:56
  45.9 7.1 %collective-permute-done.5 = bf16[128,512]{1,0:T(8,128)(2,1)S(1)} collective-permute-done((bf16[128,512]{1,0:T(8,128)(2,1)S(1)}, bf16[128,512]{1,0:T(8,128)(2,1)S(1)}, u32[]{:S(2)}, u32[]{:S(2)}) %collective-permute-start.5) | collective-permute-done | bytes 131104 | tf_op jit(solution)/shard_map/ppermute | solution.py:56
  53.7 7.1 %collective-permute-done.6 = bf16[128,512]{1,0:T(8,128)(2,1)S(1)} collective-permute-done((bf16[128,512]{1,0:T(8,128)(2,1)S(1)}, bf16[128,512]{1,0:T(8,128)(2,1)S(1)}, u32[]{:S(2)}, u32[]{:S(2)}) %collective-permute-start.6) | collective-permute-done | bytes 131104 | tf_op jit(solution)/shard_map/ppermute | solution.py:56
  61.4 7.1 %collective-permute-done.7 = bf16[128,512]{1,0:T(8,128)(2,1)S(1)} collective-permute-done((bf16[128,512]{1,0:T(8,128)(2,1)S(1)}, bf16[128,512]{1,0:T(8,128)(2,1)S(1)}, u32[]{:S(2)}, u32[]{:S(2)}) %collective-permute-start.7) | collective-permute-done | bytes 131104 | tf_op jit(solution)/shard_map/ppermute | solution.py:56
  69.1 7.1 %collective-permute-done.8 = bf16[128,512]{1,0:T(8,128)(2,1)S(1)} collective-permute-done((bf16[128,512]{1,0:T(8,128)(2,1)S(1)}, bf16[128,512]{1,0:T(8,128)(2,1)S(1)}, u32[]{:S(2)}, u32[]{:S(2)}) %collective-permute-start.8) | collective-permute-done | bytes 131104 | tf_op jit(solution)/shard_map/ppermute | solution.py:56
  76.9 7.2 %collective-permute-done.9 = bf16[128,512]{1,0:T(8,128)(2,1)} collective-permute-done((bf16[128,512]{1,0:T(8,128)(2,1)S(1)}, bf16[128,512]{1,0:T(8,128)(2,1)}, u32[]{:S(2)}, u32[]{:S(2)}) %collective-permute-start.9) | collective-permute-done | bytes 131104 | tf_op jit(solution)/shard_map/ppermute | solution.py:56
  84.1 8.8 %multiply_reduce_fusion.1 = f32[1024]{0:T(1024)S(1)} fusion(bf16[8192,1024]{1,0:T(8,128)(2,1)} %param.9, bf16[8192,128]{1,0:T(8,128)(2,1)} %param.11, bf16[2,64,1024]{2,1,0:T(8,128)(2,1)} %param.12), kind=kOutput, calls=%fused_computation.1 | convolution fusion | flops 1107295232 | bytes 19009536 | tf_op jit(solution)/shard_map/dot_general | solution.py:47
  93.0 5.4 %multiply_reduce_fusion = f32[1024]{0:T(1024)S(1)} fusion(bf16[8192,1024]{1,0:T(8,128)(2,1)S(1)} %copy-done, bf16[8192,128]{1,0:T(8,128)(2,1)S(1)} %copy-done.3, bf16[2,64,1024]{2,1,0:T(8,128)(2,1)S(1)} %copy-done.5), kind=kOutput, calls=%fused_computation | convolution fusion | flops 1107295232 | bytes 19009536 | tf_op jit(solution)/shard_map/dot_general | solution.py:47
  98.5 1.9 collective-permute-done.11
  100.4 7.3 %collective-permute-done.12 = bf16[128,512]{1,0:T(8,128)(2,1)S(1)} collective-permute-done((bf16[128,512]{1,0:T(8,128)(2,1)}, bf16[128,512]{1,0:T(8,128)(2,1)S(1)}, u32[]{:S(2)}, u32[]{:S(2)}) %collective-permute-start.12) | collective-permute-done | bytes 131104 | tf_op jit(solution)/shard_map/ppermute | solution.py:56
  107.7 7.1 %collective-permute-done.13 = bf16[128,512]{1,0:T(8,128)(2,1)S(1)} collective-permute-done((bf16[128,512]{1,0:T(8,128)(2,1)S(1)}, bf16[128,512]{1,0:T(8,128)(2,1)S(1)}, u32[]{:S(2)}, u32[]{:S(2)}) %collective-permute-start.13) | collective-permute-done | bytes 131104 | tf_op jit(solution)/shard_map/ppermute | solution.py:56
  114.8 7.1 %collective-permute-done.14 = bf16[128,512]{1,0:T(8,128)(2,1)S(1)} collective-permute-done((bf16[128,512]{1,0:T(8,128)(2,1)S(1)}, bf16[128,512]{1,0:T(8,128)(2,1)S(1)}, u32[]{:S(2)}, u32[]{:S(2)}) %collective-permute-start.14) | collective-permute-done | bytes 131104 | tf_op jit(solution)/shard_map/ppermute | solution.py:56
  122.8 0.9 constant_dynamic-update-slice_fusion.27
  124.7 0.9 constant_dynamic-update-slice_fusion.25
  126.5 0.9 constant_dynamic-update-slice_fusion.23
  135.2 1.0 convolution_convert_fusion
  136.7 9.4 %convolution_add_fusion.2 = f32[128,1024]{1,0:T(8,128)S(1)} fusion(f32[128,1024]{1,0:T(8,128)S(1)} %fusion.21, bf16[8192,1024]{1,0:T(8,128)(2,1)} %param.10, bf16[128,16384]{1,0:T(8,128)(2,1)S(1)} %constant_dynamic-update-slice_fusion, s32[]{:T(128)S(6)} %select_n.17), kind=kOutput, calls=%fused_computation.7 | convolution fusion | flops 2147614720 | bytes 19922948 | tf_op jit(solution)/shard_map/dot_general | solution.py:61
  146.1 1.2 slice-done.3
  147.3 3.6 %multiply_reduce_fusion.3 = (f32[1024]{0:T(1024)S(1)}, f32[1024]{0:T(1024)S(1)}, bf16[128,1024]{1,0:T(8,128)(2,1)S(1)}, bf16[128,1024]{1,0:T(8,128)(2,1)}, bf16[128,1024]{1,0:T(8,128)(2,1)S(1)}) fusion(f32[1024]{0:T(1024)S(1)} %bitcast.53, f32[128,1024]{1,0:T(8,128)S(1)} %convolution_add_fusion.2, f32[1024]{0:T(1024)S(1)} %bitcast.54, ...), kind=kOutput, calls=%fused_computation.32 | convolution fusion | flops 2150889472 | bytes 20987908 | tf_op jit(solution)/shard_map/dot_general | solution.py:60
  151.2 13.3 %fusion.48 = f32[128,8192]{1,0:T(8,128)} fusion(bf16[128,1024]{1,0:T(8,128)(2,1)S(1)} %get-tuple-element.14, bf16[8192,1024]{1,0:T(8,128)(2,1)} %param.9), kind=kOutput, calls=%fused_computation.110 | convolution fusion | flops 2147483648 | bytes 21233664 | tf_op jit(solution)/shard_map/dot_general | solution.py:22
  165.7 14.6 %convolution_add_fusion.1 = f32[128,8192]{1,0:T(8,128)} fusion(f32[128,8192]{1,0:T(8,128)} %fusion.48, bf16[128,1024]{1,0:T(8,128)(2,1)S(1)} %get-tuple-element.16, bf16[8192,1024]{1,0:T(8,128)(2,1)} %param.10), kind=kOutput, calls=%fused_computation.4 | convolution fusion | flops 2148532224 | bytes 25427968 | tf_op jit(solution)/shard_map/dot_general | solution.py:22
  183.3 30.0 %psum.15 = f32[]{:T(128)} all-reduce(f32[]{:T(128)S(6)} %add.111), channel_id=1, replica_groups=mesh['groups'=2,'out'=16] {'out'}, use_global_device_ids=true, to_apply=%region_8.9 | all-reduce | flops 1 | bytes 8 | tf_op jit(solution)/shard_map/psum | solution.py:96
  213.3 34.4 %all-reduce.2.cloned.1.call-done = f32[128,128]{0,1:T(8,128)} async-done(((f32[128,128]{0,1:T(8,128)}), f32[128,128]{0,1:T(8,128)}) %all-reduce.2.cloned.1.call-update) | async-done | bytes 65552 | tf_op jit(solution)/shard_map/psum | solution.py:96
  247.7 0.9 subtract_convert_fusion
  248.7 2.5 fusion.8
  251.5 1.9 fusion.3
  257.6 68.8 %reduce-scatter.2.cloned.1.call-done = f32[128,512]{1,0:T(8,128)} async-done(((f32[128,8192]{1,0:T(8,128)}), f32[128,512]{1,0:T(8,128)}) %reduce-scatter.2.cloned.1.call-update) | async-done | bytes 262160 | tf_op jit(solution)/shard_map/reduce_scatter | solution.py:94
  326.3 1.8 fusion.7
  (125 shorter events, 22.3 us)
Async XLA Ops:
  7.2 85.8 %copy-start.3 = (bf16[8192,128]{1,0:T(8,128)(2,1)S(1)}, bf16[8192,128]{1,0:T(8,128)(2,1)}, u32[]{:S(2)}) copy-start(bf16[8192,128]{1,0:T(8,128)(2,1)} %param.11) | copy-start | bytes 6291460
  7.2 85.8 %copy-start.5 = (bf16[2,64,1024]{2,1,0:T(8,128)(2,1)S(1)}, bf16[2,64,1024]{2,1,0:T(8,128)(2,1)}, u32[]{:S(2)}) copy-start(bf16[2,64,1024]{2,1,0:T(8,128)(2,1)} %param.12) | copy-start | bytes 786436
  7.2 240.5 %all-reduce.2.cloned.1.call-start = ((), (), s32[]{:S(2)}) async-start(), calls=%async_computation.2 | async-start | bytes 131072 | tf_op jit(solution)/shard_map/psum | solution.py:96
  7.2 85.8 %copy-start = (bf16[8192,1024]{1,0:T(8,128)(2,1)S(1)}, bf16[8192,1024]{1,0:T(8,128)(2,1)}, u32[]{:S(2)}) copy-start(bf16[8192,1024]{1,0:T(8,128)(2,1)} %param.10) | copy-start | bytes 50331652
  7.2 8.4 %collective-permute-start = (bf16[128,512]{1,0:T(8,128)(2,1)}, bf16[128,512]{1,0:T(8,128)(2,1)S(1)}, u32[]{:S(2)}, u32[]{:S(2)}) collective-permute-start(bf16[128,512]{1,0:T(8,128)(2,1)} %param.7), channel_id=1, source_target_pairs={{0,1},{1,2},{2,3},{3,4},{4,5},{5,6},{6,7},{7,8},{8,9},{9,10},{10,1... | collective-permute-start | bytes 393224 | tf_op jit(solution)/shard_map/ppermute | solution.py:56
  15.6 7.1 %collective-permute-start.1 = (bf16[128,512]{1,0:T(8,128)(2,1)S(1)}, bf16[128,512]{1,0:T(8,128)(2,1)S(1)}, u32[]{:S(2)}, u32[]{:S(2)}) collective-permute-start(bf16[128,512]{1,0:T(8,128)(2,1)S(1)} %collective-permute-done), channel_id=1, source_target_pairs={{0,1},{1,2},{2,3},{3,4},{4,5},{5,6},{6,7},{7,8},{8,9},{9,10},{10,1... | collective-permute-start | bytes 393224 | tf_op jit(solution)/shard_map/ppermute | solution.py:56
  22.7 61.4 %copy-start.6 = (bf16[128,512]{1,0:T(8,128)(2,1)}, bf16[128,512]{1,0:T(8,128)(2,1)S(1)}, u32[]{:S(2)}) copy-start(bf16[128,512]{1,0:T(8,128)(2,1)S(1)} %collective-permute-done.1) | copy-start | bytes 393220
  22.7 7.1 %collective-permute-start.2 = (bf16[128,512]{1,0:T(8,128)(2,1)S(1)}, bf16[128,512]{1,0:T(8,128)(2,1)S(1)}, u32[]{:S(2)}, u32[]{:S(2)}) collective-permute-start(bf16[128,512]{1,0:T(8,128)(2,1)S(1)} %collective-permute-done.1), channel_id=1, source_target_pairs={{0,1},{1,2},{2,3},{3,4},{4,5},{5,6},{6,7},{7,8},{8,9},{9,10},{10,1... | collective-permute-start | bytes 393224 | tf_op jit(solution)/shard_map/ppermute | solution.py:56
  30.4 7.1 %collective-permute-start.3 = (bf16[128,512]{1,0:T(8,128)(2,1)S(1)}, bf16[128,512]{1,0:T(8,128)(2,1)S(1)}, u32[]{:S(2)}, u32[]{:S(2)}) collective-permute-start(bf16[128,512]{1,0:T(8,128)(2,1)S(1)} %collective-permute-done.2), channel_id=1, source_target_pairs={{0,1},{1,2},{2,3},{3,4},{4,5},{5,6},{6,7},{7,8},{8,9},{9,10},{10,1... | collective-permute-start | bytes 393224 | tf_op jit(solution)/shard_map/ppermute | solution.py:56
  38.2 7.1 %collective-permute-start.4 = (bf16[128,512]{1,0:T(8,128)(2,1)S(1)}, bf16[128,512]{1,0:T(8,128)(2,1)S(1)}, u32[]{:S(2)}, u32[]{:S(2)}) collective-permute-start(bf16[128,512]{1,0:T(8,128)(2,1)S(1)} %collective-permute-done.3), channel_id=1, source_target_pairs={{0,1},{1,2},{2,3},{3,4},{4,5},{5,6},{6,7},{7,8},{8,9},{9,10},{10,1... | collective-permute-start | bytes 393224 | tf_op jit(solution)/shard_map/ppermute | solution.py:56
  45.9 7.1 %collective-permute-start.5 = (bf16[128,512]{1,0:T(8,128)(2,1)S(1)}, bf16[128,512]{1,0:T(8,128)(2,1)S(1)}, u32[]{:S(2)}, u32[]{:S(2)}) collective-permute-start(bf16[128,512]{1,0:T(8,128)(2,1)S(1)} %collective-permute-done.4), channel_id=1, source_target_pairs={{0,1},{1,2},{2,3},{3,4},{4,5},{5,6},{6,7},{7,8},{8,9},{9,10},{10,1... | collective-permute-start | bytes 393224 | tf_op jit(solution)/shard_map/ppermute | solution.py:56
  53.7 7.1 %collective-permute-start.6 = (bf16[128,512]{1,0:T(8,128)(2,1)S(1)}, bf16[128,512]{1,0:T(8,128)(2,1)S(1)}, u32[]{:S(2)}, u32[]{:S(2)}) collective-permute-start(bf16[128,512]{1,0:T(8,128)(2,1)S(1)} %collective-permute-done.5), channel_id=1, source_target_pairs={{0,1},{1,2},{2,3},{3,4},{4,5},{5,6},{6,7},{7,8},{8,9},{9,10},{10,1... | collective-permute-start | bytes 393224 | tf_op jit(solution)/shard_map/ppermute | solution.py:56
  61.4 7.1 %collective-permute-start.7 = (bf16[128,512]{1,0:T(8,128)(2,1)S(1)}, bf16[128,512]{1,0:T(8,128)(2,1)S(1)}, u32[]{:S(2)}, u32[]{:S(2)}) collective-permute-start(bf16[128,512]{1,0:T(8,128)(2,1)S(1)} %collective-permute-done.6), channel_id=1, source_target_pairs={{0,1},{1,2},{2,3},{3,4},{4,5},{5,6},{6,7},{7,8},{8,9},{9,10},{10,1... | collective-permute-start | bytes 393224 | tf_op jit(solution)/shard_map/ppermute | solution.py:56
  69.1 7.1 %collective-permute-start.8 = (bf16[128,512]{1,0:T(8,128)(2,1)S(1)}, bf16[128,512]{1,0:T(8,128)(2,1)S(1)}, u32[]{:S(2)}, u32[]{:S(2)}) collective-permute-start(bf16[128,512]{1,0:T(8,128)(2,1)S(1)} %collective-permute-done.7), channel_id=1, source_target_pairs={{0,1},{1,2},{2,3},{3,4},{4,5},{5,6},{6,7},{7,8},{8,9},{9,10},{10,1... | collective-permute-start | bytes 393224 | tf_op jit(solution)/shard_map/ppermute | solution.py:56
  76.9 7.2 %collective-permute-start.9 = (bf16[128,512]{1,0:T(8,128)(2,1)S(1)}, bf16[128,512]{1,0:T(8,128)(2,1)}, u32[]{:S(2)}, u32[]{:S(2)}) collective-permute-start(bf16[128,512]{1,0:T(8,128)(2,1)S(1)} %collective-permute-done.8), channel_id=1, source_target_pairs={{0,1},{1,2},{2,3},{3,4},{4,5},{5,6},{6,7},{7,8},{8,9},{9,10},{10,1... | collective-permute-start | bytes 393224 | tf_op jit(solution)/shard_map/ppermute | solution.py:56
  84.1 8.8 %collective-permute-start.10 = (bf16[128,512]{1,0:T(8,128)(2,1)}, bf16[128,512]{1,0:T(8,128)(2,1)}, u32[]{:S(2)}, u32[]{:S(2)}) collective-permute-start(bf16[128,512]{1,0:T(8,128)(2,1)} %collective-permute-done.9), channel_id=1, source_target_pairs={{0,1},{1,2},{2,3},{3,4},{4,5},{5,6},{6,7},{7,8},{8,9},{9,10},{10,1... | collective-permute-start | bytes 393224 | tf_op jit(solution)/shard_map/ppermute | solution.py:56
  92.9 21.9 %copy-start.22 = (f32[2,1024]{1,0:T(2,128)S(1)}, f32[2,1024]{1,0:T(2,128)}, u32[]{:S(2)}) copy-start(f32[2,1024]{1,0:T(2,128)} %param.13) | copy-start | bytes 24580
  92.9 39.1 %copy-start.4 = (bf16[128,512]{1,0:T(8,128)(2,1)S(1)}, bf16[128,512]{1,0:T(8,128)(2,1)}, u32[]{:S(2)}) copy-start(bf16[128,512]{1,0:T(8,128)(2,1)} %param.7) | copy-start | bytes 393220
  92.9 7.5 %collective-permute-start.11 = (bf16[128,512]{1,0:T(8,128)(2,1)}, bf16[128,512]{1,0:T(8,128)(2,1)}, u32[]{:S(2)}, u32[]{:S(2)}) collective-permute-start(bf16[128,512]{1,0:T(8,128)(2,1)} %collective-permute-done.10), channel_id=1, source_target_pairs={{0,1},{1,2},{2,3},{3,4},{4,5},{5,6},{6,7},{7,8},{8,9},{9,10},{10,1... | collective-permute-start | bytes 393224 | tf_op jit(solution)/shard_map/ppermute | solution.py:56
  98.4 36.5 %copy-start.17 = (bf16[128,512]{1,0:T(8,128)(2,1)S(1)}, bf16[128,512]{1,0:T(8,128)(2,1)}, u32[]{:S(2)}) copy-start(bf16[128,512]{1,0:T(8,128)(2,1)} %copy-done.16) | copy-start | bytes 393220
  98.4 36.5 %copy-start.15 = (bf16[128,512]{1,0:T(8,128)(2,1)S(1)}, bf16[128,512]{1,0:T(8,128)(2,1)}, u32[]{:S(2)}) copy-start(bf16[128,512]{1,0:T(8,128)(2,1)} %copy-done.14) | copy-start | bytes 393220
  98.4 36.6 %copy-start.13 = (bf16[128,512]{1,0:T(8,128)(2,1)S(1)}, bf16[128,512]{1,0:T(8,128)(2,1)}, u32[]{:S(2)}) copy-start(bf16[128,512]{1,0:T(8,128)(2,1)} %copy-done.12) | copy-start | bytes 393220
  98.4 36.6 %copy-start.11 = (bf16[128,512]{1,0:T(8,128)(2,1)S(1)}, bf16[128,512]{1,0:T(8,128)(2,1)}, u32[]{:S(2)}) copy-start(bf16[128,512]{1,0:T(8,128)(2,1)} %copy-done.10) | copy-start | bytes 393220
  98.5 36.6 %copy-start.9 = (bf16[128,512]{1,0:T(8,128)(2,1)S(1)}, bf16[128,512]{1,0:T(8,128)(2,1)}, u32[]{:S(2)}) copy-start(bf16[128,512]{1,0:T(8,128)(2,1)} %copy-done.8) | copy-start | bytes 393220
  98.5 36.6 %copy-start.7 = (bf16[128,512]{1,0:T(8,128)(2,1)S(1)}, bf16[128,512]{1,0:T(8,128)(2,1)}, u32[]{:S(2)}) copy-start(bf16[128,512]{1,0:T(8,128)(2,1)} %copy-done.6) | copy-start | bytes 393220
  98.5 36.4 %copy-start.21 = (bf16[128,512]{1,0:T(8,128)(2,1)S(1)}, bf16[128,512]{1,0:T(8,128)(2,1)}, u32[]{:S(2)}) copy-start(bf16[128,512]{1,0:T(8,128)(2,1)} %copy-done.20) | copy-start | bytes 393220
  98.5 36.4 %copy-start.19 = (bf16[128,512]{1,0:T(8,128)(2,1)S(1)}, bf16[128,512]{1,0:T(8,128)(2,1)}, u32[]{:S(2)}) copy-start(bf16[128,512]{1,0:T(8,128)(2,1)} %copy-done.18) | copy-start | bytes 393220
  100.4 7.3 %collective-permute-start.12 = (bf16[128,512]{1,0:T(8,128)(2,1)}, bf16[128,512]{1,0:T(8,128)(2,1)S(1)}, u32[]{:S(2)}, u32[]{:S(2)}) collective-permute-start(bf16[128,512]{1,0:T(8,128)(2,1)} %collective-permute-done.11), channel_id=1, source_target_pairs={{0,1},{1,2},{2,3},{3,4},{4,5},{5,6},{6,7},{7,8},{8,9},{9,10},{10,1... | collective-permute-start | bytes 393224 | tf_op jit(solution)/shard_map/ppermute | solution.py:56
  107.7 7.1 %collective-permute-start.13 = (bf16[128,512]{1,0:T(8,128)(2,1)S(1)}, bf16[128,512]{1,0:T(8,128)(2,1)S(1)}, u32[]{:S(2)}, u32[]{:S(2)}) collective-permute-start(bf16[128,512]{1,0:T(8,128)(2,1)S(1)} %collective-permute-done.12), channel_id=1, source_target_pairs={{0,1},{1,2},{2,3},{3,4},{4,5},{5,6},{6,7},{7,8},{8,9},{9,10},{10,1... | collective-permute-start | bytes 393224 | tf_op jit(solution)/shard_map/ppermute | solution.py:56
  114.8 7.1 %collective-permute-start.14 = (bf16[128,512]{1,0:T(8,128)(2,1)S(1)}, bf16[128,512]{1,0:T(8,128)(2,1)S(1)}, u32[]{:S(2)}, u32[]{:S(2)}) collective-permute-start(bf16[128,512]{1,0:T(8,128)(2,1)S(1)} %collective-permute-done.13), channel_id=1, source_target_pairs={{0,1},{1,2},{2,3},{3,4},{4,5},{5,6},{6,7},{7,8},{8,9},{9,10},{10,1... | collective-permute-start | bytes 393224 | tf_op jit(solution)/shard_map/ppermute | solution.py:56
  135.1 10.9 %copy-start.1 = (bf16[128,16384]{1,0:T(8,128)(2,1)}, bf16[128,16384]{1,0:T(8,128)(2,1)S(1)}, u32[]{:S(2)}) copy-start(bf16[128,16384]{1,0:T(8,128)(2,1)S(1)} %constant_dynamic-update-slice_fusion) | copy-start | bytes 12582916
  165.4 161.0 %reduce-scatter.2.cloned.1.call-start = ((), (), s32[]{:S(2)}) async-start(), calls=%async_computation.1 | async-start | bytes 4456448 | tf_op jit(solution)/shard_map/reduce_scatter | solution.py:94
  (13 other events, 58.4 us)
Sparse Core Ops, SparseCore 0:
  165.5 82.1 all-reduce.1
  252.1 74.2 reduce-scatter.1
